TPU v7x, 32 devices: a whole 2x2x4 slice. The times are simulated.
32 devices in a mesh: row: 4 (over y, core), col: 8 (over z, x).
Axes of the slice: x: 2, y: 2, z: 4, core: 2. Of those that a mesh axis runs over, the one named last changes fastest.
Arguments:
- ainv_top: float32 [4096, 4096], P('row', 'col'), may hold values from -0.25 to 0.25
- par_struct: int32 [8, 16], replicated, may hold values from 0 to 31, as said below
- par_panel: float32 [8, 16, 128, 128], P('col', 'row'), may hold values from -6 to 6
- par_linv: float32 [8, 128, 128], P('col', 'row'), may hold values from -0.0625 to 0.0625
- par_dinv: float32 [8, 128, 128], P('col', 'row'), may hold values from -192 to 192
- kid_panel: float32 [16, 16, 128, 128], P('col', 'row'), may hold values from -6 to 6
- kid_upper: float32 [16, 128, 128], P('col', 'row'), may hold values from -6 to 6
- kid_linv: float32 [16, 128, 128], P('col', 'row'), may hold values from -0.0625 to 0.0625
- kid_dinv: float32 [16, 128, 128], P('col', 'row'), may hold values from -192 to 192
Outputs:
- par_offdiag: float32 [8, 16, 128, 128], P('col', 'row')
- par_diag: float32 [8, 128, 128], P('col', 'row')
- kid_offdiag: float32 [16, 16, 128, 128], P('col', 'row')
- kid_parent: float32 [16, 128, 128], P('col', 'row')
- kid_diag: float32 [16, 128, 128], P('col', 'row')
Inputs may be any that keep to these rules, and one draw needn't show every extreme that they name: `par_struct`: in every row, entries 2j and 2j + 1 are two different ancestors among j * 4 to (j + 1) * 4 - 1.
All inputs are finite; a program needn't handle non-finite values.
Results may differ from a plain program's by a relative error of at most 0.00014.
Values sent between devices are 32-bit elements; how exact they have to be, the bound alone decides.
No kernel may reach another device: no remote copies, remote signals or barrier semaphores. Data moves between devices by JAX's collectives and lax.ppermute only.
A program may use at most 128 MiB of HBM per device.

v0:
```python
import jax
import jax.numpy as jnp
from jax import lax
from jax.sharding import PartitionSpec as P

high = lax.Precision.HIGH
highest = lax.Precision.HIGHEST


def mm(spec, *operands, precision=high):
    return jnp.einsum(spec, *operands, precision=precision)


def on_device(
    ainv_top, par_struct, par_panel, par_linv, par_dinv, kid_panel, kid_upper, kid_linv, kid_dinv
):
    grid_rows = lax.axis_size("row")
    grid_cols = lax.axis_size("col")
    my_row = lax.axis_index("row")
    my_col = lax.axis_index("col")
    width = par_panel.shape[-1]
    band_rows = width // grid_rows
    slot_share = par_panel.shape[1]
    children = kid_panel.shape[0]
    pair_width = par_struct.shape[1] // grid_cols
    tile_rows = ainv_top.shape[0] // width
    tile_cols = ainv_top.shape[1] // width
    local_tiles = ainv_top.reshape(tile_rows, width, tile_cols, width)
    pick_rows = lax.dynamic_slice_in_dim(par_struct, my_row * slot_share, slot_share, 1)
    pick_cols = lax.dynamic_slice_in_dim(par_struct, my_col * pair_width, pair_width, 1)
    pick_rows = pick_rows - my_row * tile_rows
    pick_cols = pick_cols - my_col * tile_cols
    tiles = local_tiles[pick_rows[:, :, None], :, pick_cols[:, None, :], :]
    small = jnp.concatenate([par_linv, par_dinv, kid_upper, kid_linv, kid_dinv], axis=0)
    small = lax.all_gather(small, "row", axis=1, tiled=True)
    plinv, pdinv = (small[0], small[1])
    kupper = small[2 : 2 + children]
    klinv = small[2 + children : 2 + 2 * children]
    kdinv = small[2 + 2 * children :]
    panels = jnp.concatenate([par_panel, kid_panel], axis=0)
    every = lax.all_gather(panels, "row", axis=1, tiled=True)
    moved = lax.all_to_all(tiles, "col", 0, 0, tiled=True)
    every = every.reshape(1 + children, grid_cols, pair_width, width, width)
    prod = mm("cjkab,nckbd->njad", moved, every)
    par_off = -mm("jab,bc->jac", prod[0], plinv)
    par_hat = mm("jab,bc->jac", par_panel[0], plinv)
    kid_hat = mm("njab,nbc->njac", kid_panel, klinv)
    kuphat = mm("nab,nbc->nac", kupper, klinv)
    kid_sum = prod[1:] + mm("jab,nbc->njac", par_off, kupper)
    kid_off = -mm("njab,nbc->njac", kid_sum, klinv)
    diag_part = mm("jba,jbc->ac", par_hat, par_off)
    parent_part = mm("jba,njbc->nac", par_off, kid_hat)
    hat_part = mm("njba,njbc->nac", kid_hat, kid_off)
    inner = parent_part - mm("ab,nbc->nac", diag_part, kuphat)
    edge_part = mm("nba,nbc->nac", kuphat, inner) - hat_part
    parts = jnp.concatenate([diag_part[None], parent_part, edge_part], axis=0)
    parts = parts.reshape(1 + 2 * children, grid_rows, band_rows, width)
    parts = lax.all_to_all(parts, "row", 1, 1, tiled=True)
    sums = parts.sum(axis=1)
    par_pivot = mm("ba,bc,cd->ad", plinv, pdinv, plinv)
    kid_pivot = mm("nba,nbc,ncd->nad", klinv, kdinv, klinv)
    kid_pivot = kid_pivot + mm("nba,bc,ncd->nad", kuphat, par_pivot, kuphat)
    start = my_row * band_rows
    par_diag = lax.dynamic_slice_in_dim(par_pivot, start, band_rows, 0) - sums[0]
    kid_par = -(sums[1 : 1 + children] + mm("ab,nbc->nac", par_diag, kuphat))
    kid_diag = lax.dynamic_slice_in_dim(kid_pivot, start, band_rows, 1) + sums[1 + children :]
    return (par_off[None], par_diag[None], kid_off, kid_par, kid_diag)


def solution(mesh):
    placed = (
        P("row", "col"),
        P(),
        P("col", "row", None, None),
        P("col", "row", None),
        P("col", "row", None),
        P("col", "row", None, None),
        P("col", "row", None),
        P("col", "row", None),
        P("col", "row", None),
    )
    return jax.shard_map(
        on_device,
        mesh=mesh,
        in_specs=placed,
        out_specs=(
            P("col", "row", None, None),
            P("col", "row", None),
            P("col", "row", None, None),
            P("col", "row", None),
            P("col", "row", None),
        ),
        check_vma=False,
    )
```

profile of v0, /device:TPU:0, one launch (start us, length us, event | category | flops | bytes accessed | tf_op | source)
XLA Modules:
  0.0 147.9 jit_solution(1128994719983951276)
XLA Ops:
  7.2 0.8 fusion.41
  7.9 0.8 fusion.43
  8.7 0.1 broadcast_or_fusion
  8.8 0.1 reshape.36
  8.9 2.9 %reshape.58 = f32[8,128,4,128]{3,2,1,0:T(4,128)} reshape(f32[1024,512]{1,0:T(8,128)} %param.9) | data formatting | bytes 4194304 | tf_op jit(solution)/shard_map/reshape | solution.py:28
  11.8 1.9 %copy.49 = f32[8,128,4,128]{3,1,2,0:T(8,128)S(1)} copy(f32[8,128,4,128]{3,2,1,0:T(4,128)} %reshape.58) | data formatting | bytes 4194304 | tf_op jit(solution)/shard_map/reshape | solution.py:28
  13.7 2.9 %gather_fusion = f32[64,128,128]{2,1,0:T(8,128)} fusion(f32[8,128,4,128]{3,1,2,0:T(8,128)S(1)} %copy.49, s32[64]{0:T(128)S(1)} %reshape.36), kind=kCustom, calls=%fused_computation | custom fusion | bytes 8389120 | tf_op jit(solution)/shard_map/gather | solution.py:33
  16.5 0.0 copy-start.1
  16.5 0.0 copy-start.3
  16.5 0.0 copy-start.7
  16.5 0.0 copy-start.8
  16.5 0.0 copy-start.4
  16.6 0.0 copy-start.5
  16.6 0.0 copy-start.6
  16.6 7.4 %all-to-all-start = ((f32[8,4,2,128,128]{4,3,2,1,0:T(8,128)}), f32[8,4,2,128,128]{4,3,2,1,0:T(8,128)}, u32[]{:S(2)}, u32[]{:S(2)}) async-start(f32[8,4,2,128,128]{4,3,2,1,0:T(8,128)} %bitcast.134), calls=%async_computation | async-start | bytes 8388608 | tf_op jit(solution)/shard_map/all_to_all | solution.py:42
  24.0 0.0 all-gather.2.cloned.1.call-start
  24.0 0.0 copy-done.1
  24.0 0.0 copy-done.3
  24.0 1.0 pad_maximum_fusion
  25.0 0.0 all-gather.2.cloned.1.call-update
  25.0 0.0 copy-done.7
  25.0 0.0 copy-done.8
  25.1 0.0 copy-done.4
  25.1 0.0 copy-done.5
  25.1 0.0 copy-done.6
  25.1 7.2 %all_gather.7 = f32[8,128,128]{2,1,0:T(8,128)S(1)} all-gather(f32[8,32,128]{2,1,0:T(8,128)S(1)} %constant_dynamic-update-slice_fusion), channel_id=1, replica_groups=mesh['row'=4,'col'=8] {'row'}, dimensions={1}, use_global_device_ids=true | all-gather | bytes 655360 | tf_op jit(solution)/shard_map/all_gather | solution.py:35
  32.3 0.3 fusion.24
  32.6 0.2 fusion.30
  32.8 0.2 fusion.21
  33.0 0.3 fusion.25
  33.3 0.3 convolution_bitcast_fusion.2
  33.7 0.3 fusion.17
  34.0 0.4 convolution_bitcast_fusion.1
  34.4 22.1 %all-gather.2.cloned.1.call-done = f32[3,16,128,128]{3,2,1,0:T(8,128)} async-done(((f32[3,4,128,128]{3,2,1,0:T(8,128)}), f32[3,16,128,128]{3,2,1,0:T(8,128)}) %all-gather.2.cloned.1.call-update) | async-done | bytes 3145744 | tf_op jit(solution)/shard_map/all_gather | solution.py:41
  56.5 60.8 %all-to-all-done = f32[8,4,2,128,128]{4,3,2,1,0:T(8,128)} async-done(((f32[8,4,2,128,128]{4,3,2,1,0:T(8,128)}), f32[8,4,2,128,128]{4,3,2,1,0:T(8,128)}, u32[]{:S(2)}, u32[]{:S(2)}) %all-to-all-start) | async-done | bytes 4194336 | tf_op jit(solution)/shard_map/all_to_all | solution.py:42
  117.3 7.8 %fusion.3 = f32[3,4,128,128]{2,3,1,0:T(8,128)S(1)} fusion(f32[3,8,2,128,128,1]{4,3,2,1,5,0:T(8,128)} %bitcast.136, f32[8,4,2,128,128]{4,3,2,1,0:T(8,128)} %all-to-all-done), kind=kOutput, calls=%fused_computation.4 | convolution fusion | flops 2415919104 | bytes 8126464 | tf_op jit(solution)/shard_map/cjkab,nckbd->njad/dot_general | solution.py:11
  125.1 0.4 convolution_negate_fusion.1
  125.5 0.0 copy-start
  125.5 0.4 fusion.6
  126.0 0.4 fusion.11
  126.3 0.3 fusion.45
  126.6 0.6 convolution_negate_fusion
  127.2 0.0 copy-start.2
  127.2 0.4 convolution_bitcast_fusion.3
  127.6 0.2 fusion.7
  127.8 0.3 convolution_subtract_fusion
  128.1 0.7 pad_maximum_fusion.1
  128.8 3.5 %all-to-all-start.1 = ((f32[5,4,32,128]{3,2,0,1:T(8,128)}), f32[5,4,32,128]{3,2,0,1:T(8,128)S(1)}, u32[]{:S(2)}, u32[]{:S(2)}) async-start(f32[5,4,32,128]{3,2,0,1:T(8,128)} %pad_maximum_fusion.1), calls=%async_computation.1 | async-start | bytes 655360 | tf_op jit(solution)/shard_map/all_to_all | solution.py:58
  132.3 0.2 fusion.46
  132.5 0.2 fusion.19
  132.7 0.0 copy-done
  132.7 6.3 %all-to-all-done.1 = f32[5,4,32,128]{3,2,0,1:T(8,128)S(1)} async-done(((f32[5,4,32,128]{3,2,0,1:T(8,128)}), f32[5,4,32,128]{3,2,0,1:T(8,128)S(1)}, u32[]{:S(2)}, u32[]{:S(2)}) %all-to-all-start.1) | async-done | bytes 327712 | tf_op jit(solution)/shard_map/all_to_all | solution.py:58
  139.0 0.8 fusion.9
  139.8 0.6 fusion.39
  140.4 0.6 slice_add_fusion
  141.0 0.0 copy-done.2
  (6 shorter events, 0.0 us)
Async XLA Ops:
  16.5 7.5 %copy-start.1 = (f32[2,4,128,128]{3,2,1,0:T(8,128)S(1)}, f32[2,4,128,128]{3,2,1,0:T(8,128)}, u32[]{:S(2)}) copy-start(f32[2,4,128,128]{3,2,1,0:T(8,128)} %param.14) | copy-start | bytes 1572868
  16.5 7.5 %copy-start.3 = (f32[1,4,128,128]{3,2,1,0:T(8,128)S(1)}, f32[1,4,128,128]{3,2,1,0:T(8,128)}, u32[]{:S(2)}) copy-start(f32[1,4,128,128]{3,2,1,0:T(8,128)} %param.11) | copy-start | bytes 786436
  16.5 8.5 %copy-start.7 = (f32[1,32,128]{2,1,0:T(8,128)S(1)}, f32[1,32,128]{2,1,0:T(8,128)}, u32[]{:S(2)}) copy-start(f32[1,32,128]{2,1,0:T(8,128)} %param.12) | copy-start | bytes 49156
  16.5 8.5 %copy-start.8 = (f32[1,32,128]{2,1,0:T(8,128)S(1)}, f32[1,32,128]{2,1,0:T(8,128)}, u32[]{:S(2)}) copy-start(f32[1,32,128]{2,1,0:T(8,128)} %param.13) | copy-start | bytes 49156
  16.5 8.5 %copy-start.4 = (f32[2,32,128]{2,1,0:T(8,128)S(1)}, f32[2,32,128]{2,1,0:T(8,128)}, u32[]{:S(2)}) copy-start(f32[2,32,128]{2,1,0:T(8,128)} %param.15) | copy-start | bytes 98308
  16.6 8.5 %copy-start.5 = (f32[2,32,128]{2,1,0:T(8,128)S(1)}, f32[2,32,128]{2,1,0:T(8,128)}, u32[]{:S(2)}) copy-start(f32[2,32,128]{2,1,0:T(8,128)} %param.16) | copy-start | bytes 98308
  16.6 8.5 %copy-start.6 = (f32[2,32,128]{2,1,0:T(8,128)S(1)}, f32[2,32,128]{2,1,0:T(8,128)}, u32[]{:S(2)}) copy-start(f32[2,32,128]{2,1,0:T(8,128)} %param.17) | copy-start | bytes 98308
  16.6 100.7 %all-to-all-start = ((f32[8,4,2,128,128]{4,3,2,1,0:T(8,128)}), f32[8,4,2,128,128]{4,3,2,1,0:T(8,128)}, u32[]{:S(2)}, u32[]{:S(2)}) async-start(f32[8,4,2,128,128]{4,3,2,1,0:T(8,128)} %bitcast.134), calls=%async_computation | async-start | bytes 8388608 | tf_op jit(solution)/shard_map/all_to_all | solution.py:42
  24.0 32.5 %all-gather.2.cloned.1.call-start = ((), (), s32[]{:S(2)}) async-start(), calls=%async_computation.2 | async-start | bytes 3932160 | tf_op jit(solution)/shard_map/all_gather | solution.py:41
  125.5 7.2 %copy-start = (f32[4,128,128]{2,1,0:T(8,128)}, f32[4,128,128]{2,1,0:T(8,128)S(1)}, u32[]{:S(2)}) copy-start(f32[4,128,128]{2,1,0:T(8,128)S(1)} %convolution_negate_fusion.1) | copy-start | bytes 786436
  127.2 13.8 %copy-start.2 = (f32[2,4,128,128]{3,2,1,0:T(8,128)}, f32[2,4,128,128]{3,2,1,0:T(8,128)S(1)}, u32[]{:S(2)}) copy-start(f32[2,4,128,128]{3,2,1,0:T(8,128)S(1)} %convolution_negate_fusion) | copy-start | bytes 1572868
  128.8 10.2 %all-to-all-start.1 = ((f32[5,4,32,128]{3,2,0,1:T(8,128)}), f32[5,4,32,128]{3,2,0,1:T(8,128)S(1)}, u32[]{:S(2)}, u32[]{:S(2)}) async-start(f32[5,4,32,128]{3,2,0,1:T(8,128)} %pad_maximum_fusion.1), calls=%async_computation.1 | async-start | bytes 655360 | tf_op jit(solution)/shard_map/all_to_all | solution.py:58
Sparse Core Ops, SparseCore 0:
  26.4 30.0 all-gather.1
where the time goes:
time: 148 us
  waiting for transfers between devices  89.2 us (60%)
  between operations  14.3 us (10%)
  matrix products  13.9 us (9%)
  starting transfers between devices  10.9 us (7%)
  local copies, waits for them, and re-layouts  7.82 us (5%)
  blocking collectives  7.2 us (5%)
  other arithmetic  4.55 us (3%)
    all_to_all x1, waiting for transfers between devices, on_device(): moved = lax.all_to_all(tiles, 'col', 0, 0, tiled=True)  60.8 us
    all_gather x1, waiting for transfers between devices, on_device(): every = lax.all_gather(panels, 'row', axis=1, tiled=True)  22.1 us
    dot_general x19, matrix products, mm(): return jnp.einsum(spec, *operands, precision=precision)  13.9 us
    all_to_all x1, starting transfers between devices, on_device(): moved = lax.all_to_all(tiles, 'col', 0, 0, tiled=True)  7.4 us
    all_gather x1, blocking collectives, on_device(): small = lax.all_gather(small, 'row', axis=1, tiled=True)  7.2 us
    all_to_all x1, waiting for transfers between devices, on_device(): parts = lax.all_to_all(parts, 'row', 1, 1, tiled=True)  6.27 us
    reshape x2, local copies, waits for them, and re-layouts, on_device(): local_tiles = ainv_top.reshape(tile_rows, width, tile_cols, width)  4.78 us
    all_to_all x1, starting transfers between devices, on_device(): parts = lax.all_to_all(parts, 'row', 1, 1, tiled=True)  3.45 us
  transfers between devices with their start and end apart: 3, of which 3 were waited for; matrix products, arithmetic and copies ran while one was open for 2% of the time, Pallas kernels for 0%

commit v1 on v0

--- a/solution.py
+++ b/solution.py
@@ -5,6 +5,16 @@
 
 high = lax.Precision.HIGH
 highest = lax.Precision.HIGHEST
+
+
+def turned_line(block, axis, dim):
+    size = lax.axis_size(axis)
+    held, blocks = (block, [block])
+    for _ in range(size - 1):
+        held = lax.ppermute(held, axis, [(i, (i + 1) % size) for i in range(size)])
+        blocks.insert(0, held)
+    line = jnp.concatenate(blocks, axis=dim)
+    return jnp.roll(line, (lax.axis_index(axis) + 1) * block.shape[dim], axis=dim)
 
 
 def mm(spec, *operands, precision=high):
@@ -38,7 +48,7 @@
     klinv = small[2 + children : 2 + 2 * children]
     kdinv = small[2 + 2 * children :]
     panels = jnp.concatenate([par_panel, kid_panel], axis=0)
-    every = lax.all_gather(panels, "row", axis=1, tiled=True)
+    every = turned_line(panels, "row", 1)
     moved = lax.all_to_all(tiles, "col", 0, 0, tiled=True)
     every = every.reshape(1 + children, grid_cols, pair_width, width, width)
     prod = mm("cjkab,nckbd->njad", moved, every)

time: 148 us -> 133 us (0.90)
  waiting for transfers between devices: 89.2 us -> 75.8 us
  between operations: 14.3 us -> 1.12 us
  blocking collectives: 7.2 us -> 15.1 us
  local copies, waits for them, and re-layouts: 7.82 us -> 10.8 us
  other arithmetic: 4.55 us -> 2.31 us
  matrix products: 13.9 us -> 16.1 us
    all_gather x1 -> x0, waiting for transfers between devices: 22.1 us -> none  [on_device(): every = lax.all_gather(panels, 'row', axis=1, tiled=True)]
    ppermute x0 -> x3, waiting for transfers between devices: none -> 19.2 us  [turned_line(): held = lax.ppermute(held, axis, [(i, (i + 1) % size) for i in range(size)])]
    all_to_all x1, waiting for transfers between devices: 60.8 us -> 51.2 us  [on_device(): moved = lax.all_to_all(tiles, 'col', 0, 0, tiled=True)]
    all_gather x1, blocking collectives: 7.2 us -> 15.1 us  [on_device(): small = lax.all_gather(small, 'row', axis=1, tiled=True)]
    unnamed x22 -> x47, local copies, waits for them, and re-layouts: 0.06 us -> 2.79 us
    dot_general x19, matrix products: 13.9 us -> 16.1 us  [mm(): return jnp.einsum(spec, *operands, precision=precision)]
  transfers between devices with their start and end apart: 3 -> 5, of which waited for: 3 -> 4; matrix products, arithmetic and copies ran while one was open for 2% -> 6% of each run, Pallas kernels for 0% -> 0%
where the time goes in v1:
time: 133 us; the launch traced here: 132 us
  waiting for transfers between devices  75.8 us (57%)
  matrix products  16.1 us (12%)
  blocking collectives  15.1 us (11%)
  starting transfers between devices  11.1 us (8%)
  local copies, waits for them, and re-layouts  10.8 us (8%)
  other arithmetic  2.31 us (2%)
    all_to_all x1, waiting for transfers between devices, on_device(): moved = lax.all_to_all(tiles, 'col', 0, 0, tiled=True)  51.2 us
    ppermute x3, waiting for transfers between devices, turned_line(): held = lax.ppermute(held, axis, [(i, (i + 1) % size) for i in range(size)])  19.2 us
    dot_general x19, matrix products, mm(): return jnp.einsum(spec, *operands, precision=precision)  16.1 us
    all_gather x1, blocking collectives, on_device(): small = lax.all_gather(small, 'row', axis=1, tiled=True)  15.1 us
    all_to_all x1, starting transfers between devices, on_device(): moved = lax.all_to_all(tiles, 'col', 0, 0, tiled=True)  7.4 us
    all_to_all x1, waiting for transfers between devices, on_device(): parts = lax.all_to_all(parts, 'row', 1, 1, tiled=True)  5.36 us
    reshape x2, local copies, waits for them, and re-layouts, on_device(): local_tiles = ainv_top.reshape(tile_rows, width, tile_cols, width)  4.76 us
    all_to_all x1, starting transfers between devices, on_device(): parts = lax.all_to_all(parts, 'row', 1, 1, tiled=True)  3.45 us
  transfers between devices with their start and end apart: 5, of which 4 were waited for; matrix products, arithmetic and copies ran while one was open for 6% of the time, Pallas kernels for 0%

profile of v1, /device:TPU:0, one launch (start us, length us, event | category | flops | bytes accessed | tf_op | source)
XLA Modules:
  0.0 132.4 jit_solution(9866398177197892345)
XLA Ops:
  0.6 0.0 copy-start.16
  0.6 2.9 %reshape.58 = f32[8,128,4,128]{3,2,1,0:T(4,128)} reshape(f32[1024,512]{1,0:T(8,128)} %param.9) | data formatting | bytes 4194304 | tf_op jit(solution)/shard_map/reshape | solution.py:38
  3.5 1.9 %copy.49 = f32[8,128,4,128]{3,1,2,0:T(8,128)S(1)} copy(f32[8,128,4,128]{3,2,1,0:T(4,128)} %reshape.58) | data formatting | bytes 4194304 | tf_op jit(solution)/shard_map/reshape | solution.py:38
  5.4 0.0 copy-done.16
  5.4 0.1 fusion.43
  5.5 0.1 fusion.41
  5.6 0.1 broadcast_or_fusion
  5.7 0.1 reshape.36
  5.8 2.9 %gather_fusion = f32[64,128,128]{2,1,0:T(8,128)} fusion(f32[8,128,4,128]{3,1,2,0:T(8,128)S(1)} %copy.49, s32[64]{0:T(128)S(1)} %reshape.36), kind=kCustom, calls=%fused_computation | custom fusion | bytes 8389120 | tf_op jit(solution)/shard_map/gather | solution.py:43
  8.7 0.0 copy-start.11
  8.7 0.0 copy-start.12
  8.7 0.0 copy-start.13
  8.7 7.4 %all-to-all-start = ((f32[8,4,2,128,128]{4,3,2,1,0:T(8,128)}), f32[8,4,2,128,128]{4,3,2,1,0:T(8,128)}, u32[]{:S(2)}, u32[]{:S(2)}) async-start(f32[8,4,2,128,128]{4,3,2,1,0:T(8,128)} %bitcast.134), calls=%async_computation | async-start | bytes 8388608 | tf_op jit(solution)/shard_map/all_to_all | solution.py:52
  16.1 0.0 copy-done.2
  16.1 0.1 pad_maximum_fusion
  16.2 0.1 collective-permute-start
  16.3 0.0 copy-done.15
  16.3 0.0 copy-done.11
  16.4 11.3 %collective-permute-done = f32[3,4,128,128]{3,2,1,0:T(8,128)S(1)} collective-permute-done((f32[3,4,128,128]{3,2,1,0:T(8,128)S(1)}, f32[3,4,128,128]{3,2,1,0:T(8,128)S(1)}, u32[]{:S(2)}, u32[]{:S(2)}) %collective-permute-start) | collective-permute-done | bytes 786464 | tf_op jit(solution)/shard_map/ppermute | solution.py:14
  27.6 0.0 collective-permute-start.1
  27.6 15.1 %all_gather.3 = f32[8,128,128]{2,1,0:T(8,128)S(1)} all-gather(f32[8,32,128]{2,1,0:T(8,128)S(1)} %constant_dynamic-update-slice_fusion.10), channel_id=1, replica_groups=mesh['row'=4,'col'=8] {'row'}, dimensions={1}, use_global_device_ids=true | all-gather | bytes 655360 | tf_op jit(solution)/shard_map/all_gather | solution.py:45
  42.8 0.2 fusion.24
  43.0 0.3 fusion.30
  43.3 0.2 fusion.21
  43.5 0.0 collective-permute-done.1
  43.5 0.2 collective-permute-start.2
  43.7 0.9 fusion.25
  44.7 0.3 convolution_bitcast_fusion.2
  45.0 0.9 fusion.17
  45.9 1.2 convolution_bitcast_fusion.1
  47.1 7.9 %collective-permute-done.2 = f32[3,4,128,128]{3,2,1,0:T(8,128)} collective-permute-done((f32[3,4,128,128]{3,2,1,0:T(8,128)S(1)}, f32[3,4,128,128]{3,2,1,0:T(8,128)}, u32[]{:S(2)}, u32[]{:S(2)}) %collective-permute-start.2) | collective-permute-done | bytes 786464 | tf_op jit(solution)/shard_map/ppermute | solution.py:14
  55.1 1.2 constant_dynamic-update-slice_fusion.9
  56.3 0.1 constant_dynamic-update-slice_fusion.8
  56.3 0.1 constant_dynamic-update-slice_fusion.7
  56.5 1.2 constant_dynamic-update-slice_fusion.4
  57.7 0.1 constant_dynamic-update-slice_fusion.3
  57.8 0.1 constant_dynamic-update-slice_fusion.2
  57.9 0.2 constant_dynamic-slice_fusion
  58.1 51.2 %all-to-all-done = f32[8,4,2,128,128]{4,3,2,1,0:T(8,128)} async-done(((f32[8,4,2,128,128]{4,3,2,1,0:T(8,128)}), f32[8,4,2,128,128]{4,3,2,1,0:T(8,128)}, u32[]{:S(2)}, u32[]{:S(2)}) %all-to-all-start) | async-done | bytes 4194336 | tf_op jit(solution)/shard_map/all_to_all | solution.py:52
  109.4 7.0 %fusion.3 = f32[3,4,128,128]{2,3,1,0:T(8,128)S(1)} fusion(f32[3,8,2,128,128,1]{4,3,2,1,5,0:T(8,128)S(1)} %bitcast.135, f32[8,4,2,128,128]{4,3,2,1,0:T(8,128)} %all-to-all-done), kind=kOutput, calls=%fused_computation.4 | convolution fusion | flops 2415919104 | bytes 8126464 | tf_op jit(solution)/shard_map/cjkab,nckbd->njad/dot_general | solution.py:21
  116.4 0.0 copy-done.1
  116.4 0.0 copy-start.7
  116.4 0.0 copy-start.8
  116.4 0.0 copy-start.10
  116.4 0.4 convolution_negate_fusion.1
  116.8 0.0 copy-start.4
  116.8 0.4 fusion.6
  117.3 0.3 fusion.45
  117.5 0.0 copy-done.3
  117.6 0.4 fusion.11
  118.0 0.6 convolution_negate_fusion
  118.6 0.0 copy-start.6
  118.6 0.4 convolution_bitcast_fusion.3
  119.0 0.2 fusion.7
  119.2 0.3 convolution_subtract_fusion
  119.5 0.8 pad_maximum_fusion.1
  120.2 3.5 %all-to-all-start.1 = ((f32[5,4,32,128]{3,2,0,1:T(8,128)}), f32[5,4,32,128]{3,2,0,1:T(8,128)S(1)}, u32[]{:S(2)}, u32[]{:S(2)}) async-start(f32[5,4,32,128]{3,2,0,1:T(8,128)} %pad_maximum_fusion.1), calls=%async_computation.1 | async-start | bytes 655360 | tf_op jit(solution)/shard_map/all_to_all | solution.py:68
  123.7 0.0 copy-done.7
  123.7 0.2 fusion.46
  123.9 1.1 fusion.19
  125.0 5.4 %all-to-all-done.1 = f32[5,4,32,128]{3,2,0,1:T(8,128)S(1)} async-done(((f32[5,4,32,128]{3,2,0,1:T(8,128)}), f32[5,4,32,128]{3,2,0,1:T(8,128)S(1)}, u32[]{:S(2)}, u32[]{:S(2)}) %all-to-all-start.1) | async-done | bytes 327712 | tf_op jit(solution)/shard_map/all_to_all | solution.py:68
  130.4 0.6 fusion.39
  131.0 0.8 fusion.9
  131.8 0.6 slice_add_fusion
  (28 shorter events, 0.2 us)
Async XLA Ops:
  0.6 4.8 %copy-start.16 = (s32[8,16]{1,0:T(8,128)S(1)}, s32[8,16]{1,0:T(8,128)}, u32[]{:S(2)}) copy-start(s32[8,16]{1,0:T(8,128)} %param.10) | copy-start | bytes 1540
  8.7 7.4 %copy-start.2 = (f32[2,4,128,128]{3,2,1,0:T(8,128)S(1)}, f32[2,4,128,128]{3,2,1,0:T(8,128)}, u32[]{:S(2)}) copy-start(f32[2,4,128,128]{3,2,1,0:T(8,128)} %param.14) | copy-start | bytes 1572868
  8.7 7.4 %copy-start.5 = (f32[1,4,128,128]{3,2,1,0:T(8,128)S(1)}, f32[1,4,128,128]{3,2,1,0:T(8,128)}, u32[]{:S(2)}) copy-start(f32[1,4,128,128]{3,2,1,0:T(8,128)} %param.11) | copy-start | bytes 786436
  8.7 7.6 %copy-start.14 = (f32[1,32,128]{2,1,0:T(8,128)S(1)}, f32[1,32,128]{2,1,0:T(8,128)}, u32[]{:S(2)}) copy-start(f32[1,32,128]{2,1,0:T(8,128)} %param.12) | copy-start | bytes 49156
  8.7 7.6 %copy-start.15 = (f32[1,32,128]{2,1,0:T(8,128)S(1)}, f32[1,32,128]{2,1,0:T(8,128)}, u32[]{:S(2)}) copy-start(f32[1,32,128]{2,1,0:T(8,128)} %param.13) | copy-start | bytes 49156
  8.7 7.6 %copy-start.11 = (f32[2,32,128]{2,1,0:T(8,128)S(1)}, f32[2,32,128]{2,1,0:T(8,128)}, u32[]{:S(2)}) copy-start(f32[2,32,128]{2,1,0:T(8,128)} %param.15) | copy-start | bytes 98308
  8.7 7.6 %copy-start.12 = (f32[2,32,128]{2,1,0:T(8,128)S(1)}, f32[2,32,128]{2,1,0:T(8,128)}, u32[]{:S(2)}) copy-start(f32[2,32,128]{2,1,0:T(8,128)} %param.16) | copy-start | bytes 98308
  8.7 7.6 %copy-start.13 = (f32[2,32,128]{2,1,0:T(8,128)S(1)}, f32[2,32,128]{2,1,0:T(8,128)}, u32[]{:S(2)}) copy-start(f32[2,32,128]{2,1,0:T(8,128)} %param.17) | copy-start | bytes 98308
  8.7 100.7 %all-to-all-start = ((f32[8,4,2,128,128]{4,3,2,1,0:T(8,128)}), f32[8,4,2,128,128]{4,3,2,1,0:T(8,128)}, u32[]{:S(2)}, u32[]{:S(2)}) async-start(f32[8,4,2,128,128]{4,3,2,1,0:T(8,128)} %bitcast.134), calls=%async_computation | async-start | bytes 8388608 | tf_op jit(solution)/shard_map/all_to_all | solution.py:52
  16.2 11.5 %collective-permute-start = (f32[3,4,128,128]{3,2,1,0:T(8,128)S(1)}, f32[3,4,128,128]{3,2,1,0:T(8,128)S(1)}, u32[]{:S(2)}, u32[]{:S(2)}) collective-permute-start(f32[3,4,128,128]{3,2,1,0:T(8,128)S(1)} %pad_maximum_fusion), channel_id=1, source_target_pairs={{0,8},{8,16},{16,24},{24,0},{1,9},{9,17},{17,25},{25,1},{2,10},{10... | collective-permute-start | bytes 2359304 | tf_op jit(solution)/shard_map/ppermute | solution.py:14
  27.6 15.9 %collective-permute-start.1 = (f32[3,4,128,128]{3,2,1,0:T(8,128)S(1)}, f32[3,4,128,128]{3,2,1,0:T(8,128)S(1)}, u32[]{:S(2)}, u32[]{:S(2)}) collective-permute-start(f32[3,4,128,128]{3,2,1,0:T(8,128)S(1)} %collective-permute-done), channel_id=1, source_target_pairs={{0,8},{8,16},{16,24},{24,0},{1,9},{9,17},{17,25},{25,1},{2,10},{10... | collective-permute-start | bytes 2359304 | tf_op jit(solution)/shard_map/ppermute | solution.py:14
  42.8 15.0 %copy-start = (f32[8,128,128]{2,1,0:T(8,128)}, f32[8,128,128]{2,1,0:T(8,128)S(1)}, u32[]{:S(2)}) copy-start(f32[8,128,128]{2,1,0:T(8,128)S(1)} %all_gather.3) | copy-start | bytes 1572868
  43.3 14.5 %copy-start.9 = (f32[128,128]{1,0:T(8,128)}, f32[128,128]{1,0:T(8,128)S(1)}, u32[]{:S(2)}) copy-start(f32[128,128]{1,0:T(8,128)S(1)} %fusion.30) | copy-start | bytes 196612
  43.5 11.6 %collective-permute-start.2 = (f32[3,4,128,128]{3,2,1,0:T(8,128)S(1)}, f32[3,4,128,128]{3,2,1,0:T(8,128)}, u32[]{:S(2)}, u32[]{:S(2)}) collective-permute-start(f32[3,4,128,128]{3,2,1,0:T(8,128)S(1)} %collective-permute-done.1), channel_id=1, source_target_pairs={{0,8},{8,16},{16,24},{24,0},{1,9},{9,17},{17,25},{25,1},{2,10},{10... | collective-permute-start | bytes 2359304 | tf_op jit(solution)/shard_map/ppermute | solution.py:14
  109.4 7.0 %copy-start.1 = (f32[8,128,128]{2,1,0:T(8,128)S(1)}, f32[8,128,128]{2,1,0:T(8,128)}, u32[]{:S(2)}) copy-start(f32[8,128,128]{2,1,0:T(8,128)} %copy-done) | copy-start | bytes 1572868
  109.4 8.2 %copy-start.3 = (f32[2,4,128,128]{2,3,1,0:T(8,128)S(1)}, f32[2,4,128,128]{2,3,1,0:T(8,128)}, u32[]{:S(2)}) copy-start(f32[2,4,128,128]{2,3,1,0:T(8,128)} %convolution_bitcast_fusion.1) | copy-start | bytes 1572868
  116.4 7.3 %copy-start.7 = (f32[128,2,128]{0,2,1:T(8,128)S(1)}, f32[128,2,128]{0,2,1:T(8,128)}, u32[]{:S(2)}) copy-start(f32[128,2,128]{0,2,1:T(8,128)} %fusion.25) | copy-start | bytes 393220
  116.4 7.5 %copy-start.8 = (f32[2,128,128]{1,2,0:T(8,128)S(1)}, f32[2,128,128]{1,2,0:T(8,128)}, u32[]{:S(2)}) copy-start(f32[2,128,128]{1,2,0:T(8,128)} %fusion.17) | copy-start | bytes 393220
  116.4 14.0 %copy-start.10 = (f32[128,128]{1,0:T(8,128)S(1)}, f32[128,128]{1,0:T(8,128)}, u32[]{:S(2)}) copy-start(f32[128,128]{1,0:T(8,128)} %copy-done.9) | copy-start | bytes 196612
  116.8 15.6 %copy-start.4 = (f32[4,128,128]{2,1,0:T(8,128)}, f32[4,128,128]{2,1,0:T(8,128)S(1)}, u32[]{:S(2)}) copy-start(f32[4,128,128]{2,1,0:T(8,128)S(1)} %convolution_negate_fusion.1) | copy-start | bytes 786436
  118.6 13.9 %copy-start.6 = (f32[2,4,128,128]{3,2,1,0:T(8,128)}, f32[2,4,128,128]{3,2,1,0:T(8,128)S(1)}, u32[]{:S(2)}) copy-start(f32[2,4,128,128]{3,2,1,0:T(8,128)S(1)} %convolution_negate_fusion) | copy-start | bytes 1572868
  120.2 10.2 %all-to-all-start.1 = ((f32[5,4,32,128]{3,2,0,1:T(8,128)}), f32[5,4,32,128]{3,2,0,1:T(8,128)S(1)}, u32[]{:S(2)}, u32[]{:S(2)}) async-start(f32[5,4,32,128]{3,2,0,1:T(8,128)} %pad_maximum_fusion.1), calls=%async_computation.1 | async-start | bytes 655360 | tf_op jit(solution)/shard_map/all_to_all | solution.py:68
